TPU v7x, 256 devices: a whole 4x4x8 slice. The times are simulated.
256 devices in a mesh: row: 8 (over z), col: 32 (over x, y, core).
Axes of the slice: x: 4, y: 4, z: 8, core: 2. Of those that a mesh axis runs over, the one named last changes fastest.
Arguments:
- h_values: float32 [8, 512, 4096], P('row', 'col'), as said below
- h_places: int32 [8, 512], P('row', 'col'), may hold values from 0 to 15, as said below
- h_counts: int32 [8, 32], P('row', 'col'), may hold values from 0 to 16, as said below
- p_values: float32 [8, 512, 4096], P('row', 'col'), as said below
- p_places: int32 [8, 512], P('row', 'col'), may hold values from 0 to 15, as said below
- p_counts: int32 [8, 32], P('row', 'col'), may hold values from 0 to 16, as said below
- s_values: float32 [8, 512, 4096], P('row', 'col'), as said below
- s_places: int32 [8, 512], P('row', 'col'), may hold values from 0 to 15, as said below
- s_counts: int32 [8, 32], P('row', 'col'), may hold values from 0 to 16, as said below
- x_places: int32 [8, 512], P('row', 'col'), may hold values from 0 to 15, as said below
- x_counts: int32 [8, 32], P('row', 'col'), may hold values from 0 to 16, as said below
Outputs:
- gradient: float32 [8, 512, 4096], P('row', 'col')
Inputs may be any that keep to these rules, and one draw needn't show every extreme that they name: `h_places`: in each tile the 16 entries are a permutation of the tile's positions; the first count entries are the present blocks. Every pattern is symmetric, holds every block whose block row and block column lie in the same row panel, and every block (i, j) whose cyclic block distance min(|i - j|, 64 - |i - j|) is 2 or less or exactly 32. `p_places`: as for h_places. `s_places`: as for h_places. `x_places`: as for h_places. `h_counts`: every tile whose block columns lie in its own row panel is full. `p_counts`: as for h_counts. `s_counts`: as for h_counts. `x_counts`: as for h_counts. `h_values`: the assembled H is symmetric. `p_values`: the assembled P is symmetric. `s_values`: the assembled S is symmetric.
All inputs are finite; a program needn't handle non-finite values.
Results may differ from a plain program's by a relative error of at most 0.000088.
Values sent between devices are 32-bit elements; how exact they have to be, the bound alone decides.
A program may use at most 64 MiB of HBM per device.

v0:
```python
import jax
import jax.numpy as jnp
from jax import lax
from jax.sharding import PartitionSpec as P

BS = 64
TC = 2


def from_root(value, axis, source):
    kept = jnp.where(lax.axis_index(axis) == source, value, 0).astype(value.dtype)
    return lax.psum(kept, axis)


def assemble(values, places, counts):
    blocks_in = values[0]
    capacity = blocks_in.shape[0]
    slot_ids = lax.iota(jnp.int32, capacity)
    matches = (places[0][:, None] == slot_ids[None, :]) & (slot_ids[:, None] < counts[0, 0])
    spread = jnp.dot(matches.astype(jnp.float32).T, blocks_in, precision=lax.Precision.HIGHEST)
    row_count = capacity // TC
    return (
        spread.reshape(row_count, TC, BS, BS).transpose(0, 2, 1, 3).reshape(row_count * BS, TC * BS)
    )


def expand_mask(present, row_count, col_count):
    flags = present.reshape(row_count, col_count)
    return jnp.broadcast_to(flags[:, None, :, None], (row_count, BS, col_count, BS)).reshape(
        row_count * BS, col_count * BS
    )


def tile_mask(places, counts):
    capacity = places.shape[1]
    slot_ids = lax.iota(jnp.int32, capacity)
    matches = (places[0][:, None] == slot_ids[None, :]) & (slot_ids[:, None] < counts[0, 0])
    present = jnp.sum(matches.astype(jnp.float32), axis=0)
    return expand_mask(present, capacity // TC, TC)


def tile_to_slots(tile, places, counts):
    row_count = tile.shape[0] // BS
    blocks = (
        tile.reshape(row_count, BS, TC, BS).transpose(0, 2, 1, 3).reshape(row_count * TC, BS * BS)
    )
    picked = jnp.take(blocks, places[0], axis=0)
    slot_ids = lax.iota(jnp.int32, places.shape[1])
    used = (slot_ids < counts[0, 0]).astype(jnp.float32)
    return (picked * used[:, None])[None]


def shards(
    h_values,
    h_places,
    h_counts,
    p_values,
    p_places,
    p_counts,
    s_values,
    s_places,
    s_counts,
    x_places,
    x_counts,
):
    col_index = lax.axis_index("col")
    h_tile = assemble(h_values, h_places, h_counts)
    p_tile = assemble(p_values, p_places, p_counts)
    s_tile = assemble(s_values, s_places, s_counts)
    mask_tile = tile_mask(x_places, x_counts)
    row_width = h_tile.shape[0]
    col_width = h_tile.shape[1]
    p_columns, s_columns = (
        lax.all_gather(p_tile, "row", axis=0, tiled=True),
        lax.all_gather(s_tile, "row", axis=0, tiled=True),
    )
    product = jnp.dot(
        lax.all_gather(h_tile, "col", axis=1, tiled=True),
        p_columns,
        precision=lax.Precision.HIGHEST,
    )
    y_tile = mask_tile * product
    y_panel = lax.all_gather(y_tile, "col", axis=1, tiled=True)
    x_tile = mask_tile * jnp.dot(y_panel, s_columns, precision=lax.Precision.HIGHEST)
    per_panel = row_width // col_width
    source_row = col_index // per_panel
    offset = col_index % per_panel * col_width
    y_part = lax.dynamic_slice_in_dim(y_panel, offset, col_width, 0)
    y_mirror = from_root(y_part, "row", source_row)
    far_part = lax.dot_general(
        lax.all_gather(s_tile, "col", axis=1, tiled=True),
        y_mirror,
        (((1,), (1,)), ((), ())),
        precision=lax.Precision.HIGHEST,
    )
    mirrored = mask_tile * far_part
    return tile_to_slots(x_tile + mirrored, x_places, x_counts)


def solution(mesh):
    in_specs = (
        P("row", "col", None),
        P("row", "col"),
        P("row", "col"),
        P("row", "col", None),
        P("row", "col"),
        P("row", "col"),
        P("row", "col", None),
        P("row", "col"),
        P("row", "col"),
        P("row", "col"),
        P("row", "col"),
    )
    out_specs = P("row", "col", None)
    return jax.shard_map(shards, mesh=mesh, in_specs=in_specs, out_specs=out_specs, check_vma=False)
```

profile of v0, /device:TPU:2, one launch (start us, length us, event | category | flops | bytes accessed | tf_op | source)
XLA Modules:
  0.0 405.1 jit_solution(8840308818379448259)
XLA Ops:
  6.5 0.0 copy-start
  6.5 0.0 all-gather.8.cloned.1.call-start
  7.3 1.1 dot_general.34
  8.4 0.0 copy-start.2
  8.4 1.3 convolution_bitcast_fusion.1
  9.8 0.3 copy.26
  10.0 0.9 reshape.190
  10.9 0.0 copy-start.4
  10.9 0.0 all-gather.8.cloned.1.call-update
  10.9 0.0 all-gather.6.cloned.1.call-start
  11.6 0.0 copy-done
  11.6 0.2 dot_general.31
  11.9 0.0 copy-done.2
  11.9 0.7 convolution_bitcast_fusion.2
  12.6 0.3 copy.24
  12.8 0.9 reshape.189
  13.7 0.0 all-gather.6.cloned.1.call-update
  13.7 0.0 all-gather.10.cloned.1.call-start
  14.4 0.0 copy-done.4
  14.4 0.1 convert_reduce_fusion
  14.5 0.1 broadcast_in_dim.19
  14.6 0.2 broadcast_in_dim.20
  14.8 0.3 reshape.188
  15.1 0.0 copy-start.1
  15.2 0.0 copy-start.3
  15.2 40.0 %all-gather.8.cloned.1.call-done = f32[4096,128]{0,1:T(8,128)} async-done(((f32[512,128]{0,1:T(8,128)}), f32[4096,128]{0,1:T(8,128)}) %all-gather.8.cloned.1.call-update) | async-done | bytes 2097168 | tf_op jit(solution)/shard_map/all_gather | solution.py:74
  55.1 59.1 %all-gather.6.cloned.1.call-done = f32[512,4096]{0,1:T(8,128)} async-done(((f32[512,128]{0,1:T(8,128)}), f32[512,4096]{0,1:T(8,128)}) %all-gather.6.cloned.1.call-update) | async-done | bytes 8388624 | tf_op jit(solution)/shard_map/all_gather | solution.py:78
  114.2 16.5 %convolution_multiply_fusion = f32[512,128]{1,0:T(8,128)} fusion(f32[512,128]{1,0:T(8,128)S(1)} %reshape.188, f32[512,4096]{0,1:T(8,128)} %all-gather.6.cloned.1.call-done, f32[4096,128]{0,1:T(8,128)} %all-gather.8.cloned.1.call-done), kind=kOutput, calls=%fused_computation.7 | convolution fusion | flops 3221291008 | bytes 11010048 | tf_op jit(solution)/shard_map/dot_general | solution.py:77
  130.7 0.0 all-gather.10.cloned.1.call-update
  130.8 0.0 all-gather.12.cloned.1.call-start
  131.4 0.0 copy-done.1
  131.5 0.2 dot_general.38
  131.7 0.0 copy-done.3
  131.7 0.7 convolution_bitcast_fusion
  132.4 0.3 copy.28
  132.7 0.9 reshape.191
  133.5 0.0 all-gather.12.cloned.1.call-update
  133.6 0.0 all-gather.14.cloned.1.call-start
  133.6 0.5 all-gather.14.cloned.1.call-update
  134.2 0.2 all-reduce.2.cloned.1.call-start
  134.4 60.4 %all-gather.10.cloned.1.call-done = f32[512,4096]{1,0:T(8,128)} async-done(((f32[512,128]{1,0:T(8,128)}), f32[512,4096]{1,0:T(8,128)}) %all-gather.10.cloned.1.call-update) | async-done | bytes 8388624 | tf_op jit(solution)/shard_map/all_gather | solution.py:83
  194.8 3.2 dynamic-slice_select_fusion
  198.0 0.0 all-reduce.2.cloned.1.call-update
  198.0 39.7 %all-gather.12.cloned.1.call-done = f32[4096,128]{0,1:T(8,128)} async-done(((f32[512,128]{0,1:T(8,128)}), f32[4096,128]{0,1:T(8,128)}) %all-gather.12.cloned.1.call-update) | async-done | bytes 2097168 | tf_op jit(solution)/shard_map/all_gather | solution.py:75
  237.7 9.3 %fusion.29 = f32[512,128]{1,0:T(8,128)S(1)} fusion(f32[512,4096]{1,0:T(8,128)} %all-gather.10.cloned.1.call-done, f32[4096,128]{0,1:T(8,128)} %all-gather.12.cloned.1.call-done), kind=kOutput, calls=%fused_computation.48 | convolution fusion | flops 3221225472 | bytes 10747904 | tf_op jit(solution)/shard_map/dot_general | solution.py:84
  247.0 49.5 %all-gather.14.cloned.1.call-done = f32[512,4096]{0,1:T(8,128)} async-done(((f32[512,128]{0,1:T(8,128)}), f32[512,4096]{0,1:T(8,128)}) %all-gather.14.cloned.1.call-update) | async-done | bytes 8388624 | tf_op jit(solution)/shard_map/all_gather | solution.py:91
  296.6 83.7 %all-reduce.2.cloned.1.call-done = f32[128,4096]{1,0:T(8,128)} async-done(((f32[128,4096]{1,0:T(8,128)}), f32[128,4096]{1,0:T(8,128)}) %all-reduce.2.cloned.1.call-update) | async-done | bytes 2097168 | tf_op jit(solution)/shard_map/psum | solution.py:12
  380.3 16.0 %fusion = f32[512,128]{1,0:T(8,128)S(1)} fusion(f32[512,128]{1,0:T(8,128)S(1)} %reshape.188, f32[512,128]{1,0:T(8,128)S(1)} %fusion.29, f32[512,4096]{0,1:T(8,128)} %all-gather.14.cloned.1.call-done, f32[128,4096]{1,0:T(8,128)} %all-reduce.2.cloned.1.call-done), kind=kOutput, calls=%fused_computation.6 | convolution fusion | flops 3221356544 | bytes 11272192 | tf_op jit(solution)/shard_map/dot_general | solution.py:90
  396.3 0.3 reshape.192
  396.7 0.2 reshape.193
  396.9 0.6 gather_fusion
  397.5 0.8 fusion.7
  (9 shorter events, 0.1 us)
Async XLA Ops:
  6.5 5.1 %copy-start = (f32[1,16,4096]{2,1,0:T(8,128)S(1)}, f32[1,16,4096]{2,1,0:T(8,128)}, u32[]{:S(2)}) copy-start(f32[1,16,4096]{2,1,0:T(8,128)} %param.11) | copy-start | bytes 786436
  6.5 48.6 %all-gather.8.cloned.1.call-start = ((), (), s32[]{:S(2)}) async-start(), calls=%async_computation.1 | async-start | bytes 2359296 | tf_op jit(solution)/shard_map/all_gather | solution.py:74
  8.4 3.5 copy-start.2
  10.9 3.5 copy-start.4
  10.9 103.3 %all-gather.6.cloned.1.call-start = ((), (), s32[]{:S(2)}) async-start(), calls=%async_computation | async-start | bytes 8650752 | tf_op jit(solution)/shard_map/all_gather | solution.py:78
  13.7 181.1 %all-gather.10.cloned.1.call-start = ((), (), s32[]{:S(2)}) async-start(), calls=%async_computation.2 | async-start | bytes 8650752 | tf_op jit(solution)/shard_map/all_gather | solution.py:83
  15.1 116.3 %copy-start.1 = (f32[1,16,4096]{2,1,0:T(8,128)S(1)}, f32[1,16,4096]{2,1,0:T(8,128)}, u32[]{:S(2)}) copy-start(f32[1,16,4096]{2,1,0:T(8,128)} %param.17) | copy-start | bytes 786436
  15.2 116.5 %copy-start.3 = (s32[1,16]{1,0:T(1,128)S(1)}, s32[1,16]{1,0:T(1,128)}, u32[]{:S(2)}) copy-start(s32[1,16]{1,0:T(1,128)} %param.18) | copy-start | bytes 196
  130.8 106.9 %all-gather.12.cloned.1.call-start = ((), (), s32[]{:S(2)}) async-start(), calls=%async_computation.3 | async-start | bytes 2359296 | tf_op jit(solution)/shard_map/all_gather | solution.py:75
  133.6 163.0 %all-gather.14.cloned.1.call-start = ((), (), s32[]{:S(2)}) async-start(), calls=%async_computation.4 | async-start | bytes 8650752 | tf_op jit(solution)/shard_map/all_gather | solution.py:91
  134.2 246.2 %all-reduce.2.cloned.1.call-start = ((), (), s32[]{:S(2)}) async-start(), calls=%async_computation.5 | async-start | bytes 4194304 | tf_op jit(solution)/shard_map/psum | solution.py:12
Sparse Core Ops, SparseCore 0:
  11.1 44.0 all-gather.7
  57.7 56.4 all-gather.5
  130.9 63.8 all-gather.9
  196.5 41.1 all-gather.11
  240.1 56.4 all-gather.13
  298.8 81.4 all-reduce.1
where the time goes:
time: 405 us
  waiting for transfers between devices  333 us (82%)
  matrix products  44.6 us (11%)
  between operations  16.4 us (4%)
  local copies, waits for them, and re-layouts  6.76 us (2%)
  other arithmetic  4.09 us (1%)
    psum x1, waiting for transfers between devices, from_root(): return lax.psum(kept, axis)  83.7 us
    all_gather x1, waiting for transfers between devices, shards(): y_panel = lax.all_gather(y_tile, 'col', axis=1, tiled=True)  60.4 us
    all_gather x1, waiting for transfers between devices, shards(): lax.all_gather(h_tile, 'col', axis=1, tiled=True)  59.1 us
    all_gather x1, waiting for transfers between devices, shards(): lax.all_gather(s_tile, 'col', axis=1, tiled=True)  49.5 us
    all_gather x1, waiting for transfers between devices, shards(): lax.all_gather(p_tile, 'row', axis=0, tiled=True)  40 us
    all_gather x1, waiting for transfers between devices, shards(): lax.all_gather(s_tile, 'row', axis=0, tiled=True)  39.7 us
    dot_general x1, matrix products, shards(): jnp.dot(lax.all_gather(h_tile, 'col', axis=1, tiled=True), p_columns, pre...  16.5 us
    dot_general x1, matrix products, shards(): lax.dot_general(lax.all_gather(s_tile, 'col', axis=1, tiled=True), y_mirr...  16 us
  transfers between devices with their start and end apart: 6, of which 6 were waited for; matrix products, arithmetic and copies ran while one was open for 4% of the time, Pallas kernels for 0%

commit v1 on v0

--- a/solution.py
+++ b/solution.py
@@ -9,7 +9,7 @@
 
 def from_root(value, axis, source):
     kept = jnp.where(lax.axis_index(axis) == source, value, 0).astype(value.dtype)
-    return lax.psum(kept, axis)
+    return jnp.sum(lax.all_gather(kept, axis), axis=0)
 
 
 def assemble(values, places, counts):

time: 405 us -> 496 us (1.22)
  waiting for transfers between devices: 333 us -> 415 us
  other arithmetic: 4.09 us -> 11.5 us
    all_gather x0 -> x1, waiting for transfers between devices: none -> 164 us  [from_root(): return jnp.sum(lax.all_gather(kept, axis), axis=0)]
    psum x1 -> x0, waiting for transfers between devices: 83.7 us -> none  [from_root(): return lax.psum(kept, axis)]
    reduce_sum x0 -> x1, other arithmetic: none -> 7.36 us  [from_root(): return jnp.sum(lax.all_gather(kept, axis), axis=0)]
  transfers between devices with their start and end apart: 6 -> 6, of which waited for: 6 -> 6; matrix products, arithmetic and copies ran while one was open for 4% -> 5% of each run, Pallas kernels for 0% -> 0%
where the time goes in v1:
time: 496 us; the launch traced here: 494 us
  waiting for transfers between devices  415 us (84%)
  matrix products  44.1 us (9%)
  between operations  16.4 us (3%)
  other arithmetic  11.5 us (2%)
  local copies, waits for them, and re-layouts  6.74 us (1%)
    all_gather x1, waiting for transfers between devices, from_root(): return jnp.sum(lax.all_gather(kept, axis), axis=0)  164 us
    all_gather x1, waiting for transfers between devices, shards(): y_panel = lax.all_gather(y_tile, 'col', axis=1, tiled=True)  61.2 us
    all_gather x1, waiting for transfers between devices, shards(): lax.all_gather(h_tile, 'col', axis=1, tiled=True)  59.1 us
    all_gather x1, waiting for transfers between devices, shards(): lax.all_gather(s_tile, 'col', axis=1, tiled=True)  51.6 us
    all_gather x1, waiting for transfers between devices, shards(): lax.all_gather(p_tile, 'row', axis=0, tiled=True)  40 us
    all_gather x1, waiting for transfers between devices, shards(): lax.all_gather(s_tile, 'row', axis=0, tiled=True)  39 us
    dot_general x1, matrix products, shards(): jnp.dot(lax.all_gather(h_tile, 'col', axis=1, tiled=True), p_columns, pre...  16.5 us
    dot_general x1, matrix products, shards(): lax.dot_general(lax.all_gather(s_tile, 'col', axis=1, tiled=True), y_mirr...  15.5 us
  transfers between devices with their start and end apart: 6, of which 6 were waited for; matrix products, arithmetic and copies ran while one was open for 5% of the time, Pallas kernels for 0%

profile of v1, /device:TPU:2, one launch (start us, length us, event | category | flops | bytes accessed | tf_op | source)
XLA Modules:
  0.0 494.0 jit_solution(16677526564899280164)
XLA Ops:
  6.5 0.0 copy-start
  6.5 0.0 all-gather.10.cloned.1.call-start
  7.3 1.1 dot_general.34
  8.4 0.0 copy-start.2
  8.4 1.3 convolution_bitcast_fusion.1
  9.8 0.3 copy.26
  10.0 0.9 reshape.190
  10.9 0.0 copy-start.4
  10.9 0.0 all-gather.10.cloned.1.call-update
  10.9 0.0 all-gather.8.cloned.1.call-start
  11.6 0.0 copy-done
  11.6 0.2 dot_general.31
  11.9 0.0 copy-done.2
  11.9 0.7 convolution_bitcast_fusion.2
  12.6 0.3 copy.24
  12.8 0.9 reshape.189
  13.7 0.0 all-gather.8.cloned.1.call-update
  13.7 0.0 all-gather.12.cloned.1.call-start
  14.4 0.0 copy-done.4
  14.4 0.1 convert_reduce_fusion
  14.5 0.1 broadcast_in_dim.19
  14.6 0.2 broadcast_in_dim.20
  14.8 0.3 reshape.188
  15.1 0.0 copy-start.1
  15.2 0.0 copy-start.3
  15.2 40.0 %all-gather.10.cloned.1.call-done = f32[4096,128]{0,1:T(8,128)} async-done(((f32[512,128]{0,1:T(8,128)}), f32[4096,128]{0,1:T(8,128)}) %all-gather.10.cloned.1.call-update) | async-done | bytes 2097168 | tf_op jit(solution)/shard_map/all_gather | solution.py:74
  55.1 59.1 %all-gather.8.cloned.1.call-done = f32[512,4096]{0,1:T(8,128)} async-done(((f32[512,128]{0,1:T(8,128)}), f32[512,4096]{0,1:T(8,128)}) %all-gather.8.cloned.1.call-update) | async-done | bytes 8388624 | tf_op jit(solution)/shard_map/all_gather | solution.py:78
  114.2 16.5 %convolution_multiply_fusion = f32[512,128]{1,0:T(8,128)} fusion(f32[512,128]{1,0:T(8,128)S(1)} %reshape.188, f32[512,4096]{0,1:T(8,128)} %all-gather.8.cloned.1.call-done, f32[4096,128]{0,1:T(8,128)} %all-gather.10.cloned.1.call-done), kind=kOutput, calls=%fused_computation.7 | convolution fusion | flops 3221291008 | bytes 11010048 | tf_op jit(solution)/shard_map/dot_general | solution.py:77
  130.7 0.0 all-gather.12.cloned.1.call-update
  130.8 0.0 all-gather.14.cloned.1.call-start
  131.5 0.0 copy-done.1
  131.5 0.2 dot_general.38
  131.7 0.0 copy-done.3
  131.7 0.7 convolution_bitcast_fusion
  132.4 0.3 copy.28
  132.7 0.9 reshape.191
  133.5 0.0 all-gather.14.cloned.1.call-update
  133.5 0.0 all-gather.18.cloned.1.call-start
  133.6 61.2 %all-gather.12.cloned.1.call-done = f32[512,4096]{1,0:T(8,128)} async-done(((f32[512,128]{1,0:T(8,128)}), f32[512,4096]{1,0:T(8,128)}) %all-gather.12.cloned.1.call-update) | async-done | bytes 8388624 | tf_op jit(solution)/shard_map/all_gather | solution.py:83
  194.8 3.2 dynamic-slice_select_fusion
  198.0 0.0 all-gather.18.cloned.1.call-update
  198.0 0.2 all-gather.16.cloned.1.call-start
  198.3 0.3 all-gather.16.cloned.1.call-update
  198.6 39.0 %all-gather.14.cloned.1.call-done = f32[4096,128]{0,1:T(8,128)} async-done(((f32[512,128]{0,1:T(8,128)}), f32[4096,128]{0,1:T(8,128)}) %all-gather.14.cloned.1.call-update) | async-done | bytes 2097168 | tf_op jit(solution)/shard_map/all_gather | solution.py:75
  237.7 9.3 %fusion.29 = f32[512,128]{1,0:T(8,128)S(1)} fusion(f32[512,4096]{1,0:T(8,128)} %all-gather.12.cloned.1.call-done, f32[4096,128]{0,1:T(8,128)} %all-gather.14.cloned.1.call-done), kind=kOutput, calls=%fused_computation.48 | convolution fusion | flops 3221225472 | bytes 10747904 | tf_op jit(solution)/shard_map/dot_general | solution.py:84
  247.0 163.6 %all-gather.18.cloned.1.call-done = f32[1024,4096]{1,0:T(8,128)} async-done(((f32[128,4096]{1,0:T(8,128)}), f32[1024,4096]{1,0:T(8,128)}) %all-gather.18.cloned.1.call-update) | async-done | bytes 16777232 | tf_op jit(solution)/shard_map/all_gather | solution.py:12
  410.7 7.4 %reduce_sum.19 = f32[128,4096]{1,0:T(8,128)S(1)} reduce(f32[8,128,4096]{2,1,0:T(8,128)} %bitcast.88, f32[]{:T(128)} %constant.49.clone.1), dimensions={0}, to_apply=%region_1.2 | reduce | flops 3670016 | bytes 18874372 | tf_op jit(solution)/shard_map/reduce_sum | solution.py:12
  418.0 51.6 %all-gather.16.cloned.1.call-done = f32[512,4096]{0,1:T(8,128)} async-done(((f32[512,128]{0,1:T(8,128)}), f32[512,4096]{0,1:T(8,128)}) %all-gather.16.cloned.1.call-update) | async-done | bytes 8388624 | tf_op jit(solution)/shard_map/all_gather | solution.py:91
  469.6 15.5 %fusion = f32[512,128]{1,0:T(8,128)S(1)} fusion(f32[512,128]{1,0:T(8,128)S(1)} %reshape.188, f32[512,128]{1,0:T(8,128)S(1)} %fusion.29, f32[512,4096]{0,1:T(8,128)} %all-gather.16.cloned.1.call-done, f32[128,4096]{1,0:T(8,128)S(1)} %reduce_sum.19), kind=kOutput, calls=%fused_computation.6 | convolution fusion | flops 3221356544 | bytes 11272192 | tf_op jit(solution)/shard_map/dot_general | solution.py:90
  485.2 0.3 reshape.192
  485.6 0.2 reshape.193
  485.8 0.6 gather_fusion
  486.4 0.8 fusion.7
  (9 shorter events, 0.1 us)
Async XLA Ops:
  6.5 5.1 %copy-start = (f32[1,16,4096]{2,1,0:T(8,128)S(1)}, f32[1,16,4096]{2,1,0:T(8,128)}, u32[]{:S(2)}) copy-start(f32[1,16,4096]{2,1,0:T(8,128)} %param.11) | copy-start | bytes 786436
  6.5 48.6 %all-gather.10.cloned.1.call-start = ((), (), s32[]{:S(2)}) async-start(), calls=%async_computation.1 | async-start | bytes 2359296 | tf_op jit(solution)/shard_map/all_gather | solution.py:74
  8.4 3.5 copy-start.2
  10.9 3.5 copy-start.4
  10.9 103.3 %all-gather.8.cloned.1.call-start = ((), (), s32[]{:S(2)}) async-start(), calls=%async_computation | async-start | bytes 8650752 | tf_op jit(solution)/shard_map/all_gather | solution.py:78
  13.7 181.1 %all-gather.12.cloned.1.call-start = ((), (), s32[]{:S(2)}) async-start(), calls=%async_computation.2 | async-start | bytes 8650752 | tf_op jit(solution)/shard_map/all_gather | solution.py:83
  15.1 116.3 %copy-start.1 = (f32[1,16,4096]{2,1,0:T(8,128)S(1)}, f32[1,16,4096]{2,1,0:T(8,128)}, u32[]{:S(2)}) copy-start(f32[1,16,4096]{2,1,0:T(8,128)} %param.17) | copy-start | bytes 786436
  15.2 116.5 %copy-start.3 = (s32[1,16]{1,0:T(1,128)S(1)}, s32[1,16]{1,0:T(1,128)}, u32[]{:S(2)}) copy-start(s32[1,16]{1,0:T(1,128)} %param.18) | copy-start | bytes 196
  130.8 106.9 %all-gather.14.cloned.1.call-start = ((), (), s32[]{:S(2)}) async-start(), calls=%async_computation.3 | async-start | bytes 2359296 | tf_op jit(solution)/shard_map/all_gather | solution.py:75
  133.5 277.1 %all-gather.18.cloned.1.call-start = ((), (), s32[]{:S(2)}) async-start(), calls=%async_computation.5 | async-start | bytes 18874368 | tf_op jit(solution)/shard_map/all_gather | solution.py:12
  198.0 271.6 %all-gather.16.cloned.1.call-start = ((), (), s32[]{:S(2)}) async-start(), calls=%async_computation.4 | async-start | bytes 8650752 | tf_op jit(solution)/shard_map/all_gather | solution.py:91
Sparse Core Ops, SparseCore 0:
  11.1 44.0 all-gather.9
  57.7 56.4 all-gather.7
  130.9 63.8 all-gather.11
  196.5 41.1 all-gather.13
  239.3 171.3 all-gather.17
  413.1 56.5 all-gather.15
